TPU v7x, 512 devices: a whole 4x4x16 slice. The times are simulated.
512 devices in a mesh: dp: 16 (over x, y), expert: 32 (over z, core).
Axes of the slice: x: 4, y: 4, z: 16, core: 2. Of those that a mesh axis runs over, the one named last changes fastest.
Arguments:
- tokens: bfloat16 [16384, 3584], P('expert', 'dp'), may hold values from -6 to 6
- grad_out: bfloat16 [16384, 3584], P('expert', 'dp'), may hold values from -1.796875 to 1.796875
- expert_ids: int32 [16384, 8], P('expert'), may hold values from 0 to 255, as said below
- gates: float32 [16384, 8], P('expert'), may hold values from 0.25 to 2.5
- w_gate: bfloat16 [32, 3584, 1024], P('expert', 'dp'), may hold values from -0.09375 to 0.09375
- w_up: bfloat16 [32, 3584, 1024], P('expert', 'dp'), may hold values from -0.09375 to 0.09375
- w_down: bfloat16 [32, 1024, 3584], P('expert', None, 'dp'), may hold values from -0.1875 to 0.1875
Outputs:
- mixed: bfloat16 [16384, 3584], P('expert', 'dp')
- grad_tokens: bfloat16 [16384, 3584], P('expert', 'dp')
- grad_gate: bfloat16 [32, 3584, 1024], P('expert', 'dp')
- grad_up: bfloat16 [32, 3584, 1024], P('expert', 'dp')
- grad_down: bfloat16 [32, 1024, 3584], P('expert', None, 'dp')
Inputs may be any that keep to these rules, and one draw needn't show every extreme that they name: `expert_ids`: each row names 8 different experts, at most one of them below 32. Within each aligned block of 512 rows no expert below 32 is named by more than 32 rows, and one such expert, the same in every block, is named by exactly 32 rows of every block.
All inputs are finite; a program needn't handle non-finite values.
Results may differ from a plain program's by a relative error of at most 0.029.
Values may be sent and summed in bfloat16 or wider, within the bound.
A program may use at most 64 MiB of HBM per device.

v0:
```python
import jax
import jax.numpy as jnp
from jax import lax
from jax.sharding import PartitionSpec as P


def swish_gate(value):
    return value * jax.nn.sigmoid(value)


def swish_slope(value):
    logistic = jax.nn.sigmoid(value)
    return logistic * (1.0 + value * (1.0 - logistic))


def contract_rows(left, right):
    return lax.dot_general(
        left, right, (((0,), (0,)), ((), ())), preferred_element_type=jnp.float32
    )


def contract_cols(left, right):
    return lax.dot_general(
        left, right, (((1,), (1,)), ((), ())), preferred_element_type=jnp.float32
    )


def body(tokens, grad_out, expert_ids, gates, w_gate, w_up, w_down):
    experts = lax.axis_size("expert")
    tok_rows, features = tokens.shape
    capacity = tok_rows // 16
    slot_count = experts * capacity
    in_window = expert_ids < experts
    routed = jnp.any(in_window, axis=1)
    chosen = jnp.sum(jnp.where(in_window, expert_ids, 0), axis=1)
    weight_tok = jnp.sum(jnp.where(in_window, gates, jnp.zeros_like(gates)), axis=1)
    one_hot = (
        (chosen[:, None] == jnp.arange(experts, dtype=jnp.int32)[None, :]) & routed[:, None]
    ).astype(jnp.int32)
    position = jnp.sum((jnp.cumsum(one_hot, axis=0) - one_hot) * one_hot, axis=1)
    slot_index = jnp.where(routed, chosen * capacity + position, slot_count)
    source_row = jnp.full((slot_count,), tok_rows, jnp.int32)
    source_row = source_row.at[slot_index].set(jnp.arange(tok_rows, dtype=jnp.int32), mode="drop")
    scaled = (weight_tok[:, None] * grad_out.astype(jnp.float32)).astype(jnp.bfloat16)
    send_tokens = jnp.take(tokens, source_row, axis=0, mode="fill", fill_value=0).reshape(
        experts, capacity, features
    )
    send_grads = jnp.take(scaled, source_row, axis=0, mode="fill", fill_value=0).reshape(
        experts, capacity, features
    )
    arrived_tokens, arrived_grads = (
        lax.all_to_all(send_tokens, "expert", split_axis=0, concat_axis=0, tiled=True),
        lax.all_to_all(send_grads, "expert", split_axis=0, concat_axis=0, tiled=True),
    )
    expert_rows = arrived_tokens.reshape(slot_count, features)
    grad_rows_in = arrived_grads.reshape(slot_count, features)
    gate_mat = w_gate[0]
    up_mat = w_up[0]
    down_mat = w_down[0]
    part_gate = jnp.dot(expert_rows, gate_mat, preferred_element_type=jnp.float32)
    part_up = jnp.dot(expert_rows, up_mat, preferred_element_type=jnp.float32)
    gate_pre, up_pre = (
        lax.psum(part_gate.astype(jnp.bfloat16), "dp").astype(jnp.float32),
        lax.psum(part_up.astype(jnp.bfloat16), "dp").astype(jnp.float32),
    )
    full_act = (swish_gate(gate_pre) * up_pre).astype(jnp.bfloat16)
    expert_out = jnp.dot(full_act, down_mat, preferred_element_type=jnp.float32).astype(
        jnp.bfloat16
    )
    out_blocks = expert_out.reshape(experts, capacity, features)
    back_out = lax.all_to_all(out_blocks, "expert", split_axis=0, concat_axis=0, tiled=True)
    grad_down = contract_rows(full_act, grad_rows_in).astype(jnp.bfloat16)
    part_act = contract_cols(grad_rows_in, down_mat)
    grad_act = lax.psum(part_act.astype(jnp.bfloat16), "dp").astype(jnp.float32)
    grad_gate_pre = (grad_act * up_pre * swish_slope(gate_pre)).astype(jnp.bfloat16)
    grad_up_pre = (grad_act * swish_gate(gate_pre)).astype(jnp.bfloat16)
    grad_gate = contract_rows(expert_rows, grad_gate_pre).astype(jnp.bfloat16)
    grad_up = contract_rows(expert_rows, grad_up_pre).astype(jnp.bfloat16)
    row_grad = (contract_cols(grad_gate_pre, gate_mat) + contract_cols(grad_up_pre, up_mat)).astype(
        jnp.bfloat16
    )
    grad_blocks = row_grad.reshape(experts, capacity, features)
    back_grad = lax.all_to_all(grad_blocks, "expert", split_axis=0, concat_axis=0, tiled=True)
    token_out = jnp.take(
        back_out.reshape(slot_count, features), slot_index, axis=0, mode="fill", fill_value=0
    )
    mixed = (weight_tok[:, None] * token_out.astype(jnp.float32)).astype(jnp.bfloat16)
    grad_tokens = jnp.take(
        back_grad.reshape(slot_count, features), slot_index, axis=0, mode="fill", fill_value=0
    )
    return (mixed, grad_tokens, grad_gate[None], grad_up[None], grad_down[None])


def solution(mesh):
    placed = (
        P("expert", "dp"),
        P("expert", "dp"),
        P("expert", None),
        P("expert", None),
        P("expert", "dp", None),
        P("expert", "dp", None),
        P("expert", None, "dp"),
    )
    return jax.shard_map(
        body,
        mesh=mesh,
        in_specs=placed,
        out_specs=(
            P("expert", "dp"),
            P("expert", "dp"),
            P("expert", "dp", None),
            P("expert", "dp", None),
            P("expert", None, "dp"),
        ),
        check_vma=False,
    )
```

profile of v0, /device:TPU:1, one launch (start us, length us, event | category | flops | bytes accessed | tf_op | source)
XLA Modules:
  0.0 363.5 jit_solution(16019415011018475140)
XLA Ops:
  7.2 0.8 select_reduce_fusion
  8.7 1.2 reduce-window.6
  10.3 2.4 scatter_custom_fusion
  13.5 1.1 copy.21
  14.6 1.1 copy.19
  15.8 3.9 %gather_fusion.2 = bf16[1024,224]{1,0:T(8,128)(2,1)S(1)} fusion(bf16[512,224]{1,0:T(8,128)(2,1)S(1)} %multiply_convert_fusion, s32[1024]{0:T(1024)S(1)} %fusion.26), kind=kCustom, calls=%fused_computation.2.clone | custom fusion | bytes 921600 | tf_op jit(solution)/shard_map/jit(_take)/gather | solution.py:48
  19.8 3.9 %gather_fusion = bf16[1024,224]{1,0:T(8,128)(2,1)S(1)} fusion(bf16[512,224]{1,0:T(8,128)(2,1)S(1)} %copy.19, s32[1024]{0:T(1024)S(1)} %fusion.26), kind=kCustom, calls=%fused_computation.clone | custom fusion | bytes 921600 | tf_op jit(solution)/shard_map/jit(_take)/gather | solution.py:45
  23.7 1.0 broadcast_select_fusion
  24.7 50.0 %all_to_all.20 = bf16[32,32,224]{2,1,0:T(8,128)(2,1)S(1)} all-to-all(bf16[32,32,224]{2,1,0:T(8,128)(2,1)S(1)} %bitcast.73), channel_id=1, replica_groups=mesh['dp'=16,'expert'=32] {'expert'}, dimensions={0} | all-to-all | bytes 917504 | tf_op jit(solution)/shard_map/all_to_all | solution.py:52
  74.8 4.0 %all-to-all-start.2 = ((bf16[32,32,224]{2,1,0:T(8,128)(2,1)}), bf16[32,32,224]{2,1,0:T(8,128)(2,1)S(1)}, u32[]{:S(2)}, u32[]{:S(2)}) async-start(bf16[32,32,224]{2,1,0:T(8,128)(2,1)} %bitcast.12), calls=%async_computation.2 | async-start | bytes 1048576 | tf_op jit(solution)/shard_map/all_to_all | solution.py:53
  78.9 2.1 convolution_convert_fusion.1
  81.0 2.0 convolution_convert_fusion.2
  83.0 29.4 %all-to-all-done.2 = bf16[32,32,224]{2,1,0:T(8,128)(2,1)S(1)} async-done(((bf16[32,32,224]{2,1,0:T(8,128)(2,1)}), bf16[32,32,224]{2,1,0:T(8,128)(2,1)S(1)}, u32[]{:S(2)}, u32[]{:S(2)}) %all-to-all-start.2) | async-done | bytes 458784 | tf_op jit(solution)/shard_map/all_to_all | solution.py:53
  112.4 2.0 convolution_convert_fusion
  114.4 144.9 %all-reduce.3.cloned.1.call-done = (bf16[1024,1024]{1,0:T(8,128)(2,1)}, bf16[1024,1024]{1,0:T(8,128)(2,1)}, bf16[1024,1024]{1,0:T(8,128)(2,1)}) async-done(((bf16[1024,1024]{1,0:T(8,128)(2,1)}, bf16[1024,1024]{1,0:T(8,128)(2,1)}, bf16[1024,1024]{1,0:T(8,128)(2,1)}), (bf16[1024,1024]{1,0:T(8,128)(2,1)}, bf16[1024,1024]{1,0:T(8,128)(2,1)}, bf16[1024,1024]{1,0:T(8,128)(2,1)})) %all-reduce.3.cloned.1.call-update) | async-done | bytes 6291472 | tf_op jit(solution)/shard_map/psum | solution.py:64
  259.4 5.6 %fusion.3 = (bf16[1024,1024]{1,0:T(8,128)(2,1)S(1)}, bf16[1024,1024]{1,0:T(8,128)(2,1)S(1)}, bf16[1024,1024]{1,0:T(8,128)(2,1)}) fusion(bf16[1024,1024]{1,0:T(8,128)(2,1)} %get-tuple-element.19, bf16[1024,1024]{1,0:T(8,128)(2,1)} %get-tuple-element.18, bf16[1024,1024]{1,0:T(8,128)(2,1)} %get-tuple-element.17), kind=kLoop, calls=%fused_computation.14 | loop fusion | flops 18874368 | bytes 12582912 | tf_op jit(solution)/shard_map/convert_element_type | solution.py:76
  265.0 0.8 fusion.17
  266.3 0.8 fusion.9
  267.1 1.0 copy.22
  268.1 13.0 %all-to-all-start.3 = ((bf16[32,32,224]{2,1,0:T(8,128)(2,1)}), bf16[32,32,224]{2,1,0:T(8,128)(2,1)S(1)}, u32[]{:S(2)}, u32[]{:S(2)}) async-start(bf16[32,32,224]{2,1,0:T(8,128)(2,1)} %bitcast.70), calls=%async_computation.3 | async-start | bytes 1048576 | tf_op jit(solution)/shard_map/all_to_all | solution.py:83
  281.1 2.5 convolution_convert_fusion.6
  283.6 1.0 copy.20
  284.6 30.0 %all-to-all-done.3 = bf16[32,32,224]{2,1,0:T(8,128)(2,1)S(1)} async-done(((bf16[32,32,224]{2,1,0:T(8,128)(2,1)}), bf16[32,32,224]{2,1,0:T(8,128)(2,1)S(1)}, u32[]{:S(2)}, u32[]{:S(2)}) %all-to-all-start.3) | async-done | bytes 458784 | tf_op jit(solution)/shard_map/all_to_all | solution.py:83
  314.6 4.7 %all-to-all-start.1 = ((bf16[32,32,224]{2,1,0:T(8,128)(2,1)}), bf16[32,32,224]{2,1,0:T(8,128)(2,1)}, u32[]{:S(2)}, u32[]{:S(2)}) async-start(bf16[32,32,224]{2,1,0:T(8,128)(2,1)} %bitcast.69), calls=%async_computation.1 | async-start | bytes 1048576 | tf_op jit(solution)/shard_map/all_to_all | solution.py:71
  319.4 3.2 fusion.10
  322.6 1.4 fusion.11
  324.6 1.5 fusion.12
  326.0 1.9 gather_fusion.3
  328.1 0.8 copy.24
  328.9 24.0 %all-to-all-done.1 = bf16[32,32,224]{2,1,0:T(8,128)(2,1)} async-done(((bf16[32,32,224]{2,1,0:T(8,128)(2,1)}), bf16[32,32,224]{2,1,0:T(8,128)(2,1)}, u32[]{:S(2)}, u32[]{:S(2)}) %all-to-all-start.1) | async-done | bytes 458784 | tf_op jit(solution)/shard_map/all_to_all | solution.py:71
  352.9 2.7 gather_fusion.1
  355.8 0.8 copy.23
  (37 shorter events, 3.5 us)
Async XLA Ops:
  7.2 73.8 %copy-start = (bf16[1,224,1024]{2,1,0:T(8,128)(2,1)S(1)}, bf16[1,224,1024]{2,1,0:T(8,128)(2,1)}, u32[]{:S(2)}) copy-start(bf16[1,224,1024]{2,1,0:T(8,128)(2,1)} %param.15) | copy-start | bytes 1376260
  23.7 55.2 %copy-start.7 = (bf16[1,224,1024]{2,1,0:T(8,128)(2,1)S(1)}, bf16[1,224,1024]{2,1,0:T(8,128)(2,1)}, u32[]{:S(2)}) copy-start(bf16[1,224,1024]{2,1,0:T(8,128)(2,1)} %param.16) | copy-start | bytes 1376260
  74.8 8.2 %copy-start.2 = (bf16[32,32,224]{2,1,0:T(8,128)(2,1)}, bf16[32,32,224]{2,1,0:T(8,128)(2,1)S(1)}, u32[]{:S(2)}) copy-start(bf16[32,32,224]{2,1,0:T(8,128)(2,1)S(1)} %all_to_all.20) | copy-start | bytes 1376260
  74.8 37.6 %all-to-all-start.2 = ((bf16[32,32,224]{2,1,0:T(8,128)(2,1)}), bf16[32,32,224]{2,1,0:T(8,128)(2,1)S(1)}, u32[]{:S(2)}, u32[]{:S(2)}) async-start(bf16[32,32,224]{2,1,0:T(8,128)(2,1)} %bitcast.12), calls=%async_computation.2 | async-start | bytes 1048576 | tf_op jit(solution)/shard_map/all_to_all | solution.py:53
  78.8 180.5 %all-reduce.3.cloned.1.call-start = ((), (), s32[]{:S(2)}) async-start(), calls=%async_computation.4 | async-start | bytes 12582912 | tf_op jit(solution)/shard_map/psum | solution.py:64
  81.0 31.4 %copy-start.8 = (bf16[1,1024,224]{1,2,0:T(8,128)(2,1)S(1)}, bf16[1,1024,224]{1,2,0:T(8,128)(2,1)}, u32[]{:S(2)}) copy-start(bf16[1,1024,224]{1,2,0:T(8,128)(2,1)} %param.17) | copy-start | bytes 1376260
  112.4 2.0 copy-start.4
  265.0 1.3 copy-start.1
  268.1 46.5 %all-to-all-start.3 = ((bf16[32,32,224]{2,1,0:T(8,128)(2,1)}), bf16[32,32,224]{2,1,0:T(8,128)(2,1)S(1)}, u32[]{:S(2)}, u32[]{:S(2)}) async-start(bf16[32,32,224]{2,1,0:T(8,128)(2,1)} %bitcast.70), calls=%async_computation.3 | async-start | bytes 1048576 | tf_op jit(solution)/shard_map/all_to_all | solution.py:83
  314.6 38.3 %all-to-all-start.1 = ((bf16[32,32,224]{2,1,0:T(8,128)(2,1)}), bf16[32,32,224]{2,1,0:T(8,128)(2,1)}, u32[]{:S(2)}, u32[]{:S(2)}) async-start(bf16[32,32,224]{2,1,0:T(8,128)(2,1)} %bitcast.69), calls=%async_computation.1 | async-start | bytes 1048576 | tf_op jit(solution)/shard_map/all_to_all | solution.py:71
  319.3 3.3 copy-start.3
  322.6 1.4 copy-start.5
  322.6 1.9 copy-start.6
Sparse Core Ops, SparseCore 0:
  114.5 144.7 all-reduce.2
where the time goes:
time: 364 us; the launch traced here: 363 us
  waiting for transfers between devices  228 us (63%)
  blocking collectives  50 us (14%)
  local copies, waits for them, and re-layouts  22 us (6%)
  starting transfers between devices  21.8 us (6%)
  matrix products  16.2 us (4%)
  between operations  14.3 us (4%)
  other arithmetic  10.7 us (3%)
    psum x1, waiting for transfers between devices, body(): lax.psum(part_up.astype(jnp.bfloat16), 'dp').astype(jnp.float32)  145 us
    all_to_all x1, blocking collectives, body(): lax.all_to_all(send_tokens, 'expert', split_axis=0, concat_axis=0, tiled=...  50 us
    all_to_all x1, waiting for transfers between devices, body(): lax.all_to_all(grad_blocks, 'expert', split_axis=0, concat_axis=0, tiled=...  30 us
    all_to_all x1, waiting for transfers between devices, body(): lax.all_to_all(send_grads, 'expert', split_axis=0, concat_axis=0, tiled=T...  29.4 us
    all_to_all x1, waiting for transfers between devices, body(): lax.all_to_all(out_blocks, 'expert', split_axis=0, concat_axis=0, tiled=T...  24 us
    all_to_all x1, starting transfers between devices, body(): lax.all_to_all(grad_blocks, 'expert', split_axis=0, concat_axis=0, tiled=...  13 us
  transfers between devices with their start and end apart: 4, of which 4 were waited for; matrix products, arithmetic and copies ran while one was open for 5% of the time, Pallas kernels for 0%

commit v1 on v0

v1 whole, which is shorter than its diff:
```python
import functools

import jax
import jax.numpy as jnp
from jax import lax
from jax.experimental import pallas as pl
from jax.experimental.pallas import tpu as pltpu
from jax.sharding import PartitionSpec as P

MESH = pl.DeviceIdType.MESH
BF16 = jnp.bfloat16
F32 = jnp.float32
RING = 4
LAG = 3


def dot(left, right, dims):
    return lax.dot_general(left, right, (dims, ((), ())), preferred_element_type=F32)


def wait_bytes(ref, sem):
    pltpu.make_async_copy(ref, ref, sem).wait()


def kernel(
    experts,
    cap,
    chunks,
    tok_ref,
    gout_ref,
    ids_ref,
    gates_ref,
    wg_ref,
    wu_ref,
    wd_ref,
    mixed_ref,
    gtok_ref,
    ggate_ref,
    gup_ref,
    gdown_ref,
    send,
    recv,
    part,
    ra1,
    rb1,
    red,
    ra2,
    rb2,
    full,
    ret,
    back,
    pick,
    acc_g,
    acc_u,
    acc_d,
    disp_send,
    disp_recv,
    back_send,
    back_recv,
    xy_send,
    ra1_sem,
    rb1_sem,
    ra2_sem,
    rb2_sem,
    ag2_sem,
    ag1_sem,
):
    dp = lax.axis_index("dp")
    me = lax.axis_index("expert")
    px, py = dp // RING, dp % RING
    zs = experts // 2
    z, core = me // 2, me % 2
    per = zs // chunks
    blocks = 2 * per
    rows = blocks * cap
    toks, feat = tok_ref.shape
    slots = experts * cap
    col = part.shape[-1]
    q2 = red.shape[-2]

    def peer(dz, dc):
        return ((z + dz) % zs) * 2 + (core if dc == 0 else 1 - core)

    def x_peer(step):
        return ((px + step) % RING) * RING + py

    def y_peer(step):
        return px * RING + (py + step) % RING

    barrier = pltpu.get_barrier_semaphore()
    for dz in range(zs):
        for dc in range(2):
            if dz or dc:
                pl.semaphore_signal(
                    barrier, inc=1, device_id=(dp, peer(dz, dc)), device_id_type=MESH
                )
    for near in (x_peer(1), x_peer(RING - 1), y_peer(1), y_peer(RING - 1)):
        pl.semaphore_signal(barrier, inc=1, device_id=(near, me), device_id_type=MESH)

    ids = ids_ref[...]
    inside = ids < experts
    chosen = jnp.sum(jnp.where(inside, ids, 0).astype(F32), axis=1, keepdims=True)
    routed = jnp.sum(jnp.where(inside, 1.0, 0.0), axis=1, keepdims=True)
    weight = jnp.sum(jnp.where(inside, gates_ref[...], 0.0), axis=1, keepdims=True)
    lane_e = lax.broadcasted_iota(jnp.int32, (toks, experts), 1).astype(F32)
    one_hot = jnp.where((lane_e == chosen) & (routed > 0.0), 1.0, 0.0)
    earlier = jnp.where(
        lax.broadcasted_iota(jnp.int32, (toks, toks), 1)
        < lax.broadcasted_iota(jnp.int32, (toks, toks), 0),
        1.0,
        0.0,
    ).astype(BF16)
    counts = dot(earlier, one_hot.astype(BF16), ((1,), (0,)))
    position = jnp.sum(counts * one_hot, axis=1, keepdims=True)
    slot = jnp.where(routed > 0.0, chosen * cap + position, 2.0 * slots)
    lane_s = lax.broadcasted_iota(jnp.int32, (toks, slots), 1).astype(F32)
    pick[...] = jnp.where(lane_s == slot, 1.0, 0.0).astype(BF16)
    slot_row = jnp.broadcast_to(slot, (toks, 128)).T[0:1, :]
    sub_s = lax.broadcasted_iota(jnp.int32, (slots, toks), 0).astype(F32)
    place = jnp.where(sub_s == slot_row, 1.0, 0.0).astype(BF16)
    scaled = (weight * gout_ref[...].astype(F32)).astype(BF16)
    send[:, 0:cap, :] = (
        dot(place, tok_ref[...], ((1,), (0,))).astype(BF16).reshape(experts, cap, feat)
    )
    send[:, cap : 2 * cap, :] = (
        dot(place, scaled, ((1,), (0,))).astype(BF16).reshape(experts, cap, feat)
    )

    pl.semaphore_wait(barrier, 2 * zs - 1 + 4)

    for c in range(chunks):
        for j in range(per):
            for dc in range(2):
                dz = chunks * j + c
                target = recv.at[c, 2 * j + dc]
                if dz == 0 and dc == 0:
                    pltpu.make_async_copy(send.at[me], target, disp_recv.at[c]).start()
                else:
                    there = peer(zs - dz, dc)
                    pltpu.make_async_remote_copy(
                        src_ref=send.at[there],
                        dst_ref=target,
                        send_sem=disp_send,
                        recv_sem=disp_recv.at[c],
                        device_id=(dp, there),
                        device_id_type=MESH,
                    ).start()

    acc_g[...] = jnp.zeros_like(acc_g)
    acc_u[...] = jnp.zeros_like(acc_u)
    acc_d[...] = jnp.zeros_like(acc_d)

    def hop(src, dst, send_sem, recv_sem, near):
        pltpu.make_async_remote_copy(
            src_ref=src,
            dst_ref=dst,
            send_sem=send_sem,
            recv_sem=recv_sem,
            device_id=(near, me),
            device_id_type=MESH,
        ).start()

    first = ((px, x_peer(1), x_peer(RING - 1)), (py, y_peer(1), y_peer(RING - 1)))
    second = (first[1], first[0])

    def rs_start(src, ra, rb, c, h, ring, ssem, ra_sem, rb_sem):
        p, right, left = ring
        lo, hi = 2 * h, 2 * h + 1
        hop(src.at[c, lo, (p + 2) % 4], ra.at[c, h, 0], ssem, ra_sem.at[c, h, 0], right)
        hop(src.at[c, hi, (p + 2) % 4], ra.at[c, h, 1], ssem, ra_sem.at[c, h, 1], left)
        hop(src.at[c, hi, (p + 1) % 4], rb.at[c, h, 0], ssem, rb_sem.at[c, h], right)
        hop(src.at[c, lo, (p + 3) % 4], rb.at[c, h, 1], ssem, rb_sem.at[c, h], left)

    def rs_relay(src, ra, rb, c, h, ring, ssem, ra_sem, rb_sem):
        p, right, left = ring
        for side, b, t, near in ((0, 2 * h, (p + 1) % 4, right), (1, 2 * h + 1, (p + 3) % 4, left)):
            wait_bytes(ra.at[c, h, side], ra_sem.at[c, h, side])
            src[c, b, t] = (src[c, b, t].astype(F32) + ra[c, h, side].astype(F32)).astype(BF16)
            hop(src.at[c, b, t], rb.at[c, h, 2 + side], ssem, rb_sem.at[c, h], near)

    def rs_final(src, rb, c, h, ring, rb_sem):
        p = ring[0]
        wait_bytes(rb.at[c, h], rb_sem.at[c, h])
        lo = src[c, 2 * h, p].astype(F32) + rb[c, h, 1].astype(F32) + rb[c, h, 2].astype(F32)
        hi = src[c, 2 * h + 1, p].astype(F32) + rb[c, h, 0].astype(F32) + rb[c, h, 3].astype(F32)
        return lo, hi

    def stage_partials(c):
        wait_bytes(recv.at[c], disp_recv.at[c])
        x = recv[c, :, 0:cap, :].reshape(rows, feat)
        g = recv[c, :, cap : 2 * cap, :].reshape(rows, feat)
        for h in range(2):
            for b in (2 * h, 2 * h + 1):
                cols = slice(b * col, (b + 1) * col)
                terms = (
                    dot(x, wg_ref[:, cols], ((1,), (0,))),
                    dot(x, wu_ref[:, cols], ((1,), (0,))),
                    dot(g, wd_ref[cols, :], ((1,), (1,))),
                )
                for a in range(3):
                    part[c, b, :, a] = terms[a].astype(BF16).reshape(4, rows // 4, col)
            rs_start(part, ra1, rb1, c, h, first[h], xy_send.at[c, 0], ra1_sem, rb1_sem)

    def stage_relay1(c):
        for h in range(2):
            rs_relay(part, ra1, rb1, c, h, first[h], xy_send.at[c, 0], ra1_sem, rb1_sem)

    def stage_second(c):
        for h in range(2):
            sums = rs_final(part, rb1, c, h, first[h], rb1_sem)
            for side in range(2):
                for a in range(3):
                    red[c, 2 * h + side, :, a] = sums[side][a].astype(BF16).reshape(4, q2, col)
            rs_start(red, ra2, rb2, c, h, second[h], xy_send.at[c, 1], ra2_sem, rb2_sem)

    def stage_relay2(c):
        for h in range(2):
            rs_relay(red, ra2, rb2, c, h, second[h], xy_send.at[c, 1], ra2_sem, rb2_sem)

    def stage_pointwise(c):
        for h in range(2):
            p1 = first[h][0]
            p2, right, left = second[h]
            sums = rs_final(red, rb2, c, h, second[h], rb2_sem)
            for side in range(2):
                gate, up, grad = sums[side][0], sums[side][1], sums[side][2]
                logistic = 1.0 / (1.0 + jnp.exp(-gate))
                swish = gate * logistic
                full[c, h, p1, p2, side, 0] = (swish * up).astype(BF16)
                full[c, h, p1, p2, side, 1] = (
                    grad * up * (logistic * (1.0 + gate * (1.0 - logistic)))
                ).astype(BF16)
                full[c, h, p1, p2, side, 2] = (grad * swish).astype(BF16)
            own = full.at[c, h, p1, p2]
            hop(own, own, xy_send.at[c, 2], ag2_sem.at[c, h, 0], right)
            hop(own, own, xy_send.at[c, 2], ag2_sem.at[c, h, 1], left)

    def stage_forward2(c):
        for h in range(2):
            p1 = first[h][0]
            p2, right, left = second[h]
            for side, t, near in ((0, (p2 + 3) % 4, right), (1, (p2 + 1) % 4, left)):
                wait_bytes(full.at[c, h, p1, t], ag2_sem.at[c, h, side])
                piece = full.at[c, h, p1, t, side]
                hop(piece, piece, xy_send.at[c, 2], ag2_sem.at[c, h, 2], near)

    def stage_first(c):
        for h in range(2):
            p1, right, left = first[h]
            p2 = second[h][0]
            wait_bytes(full.at[c, h, p1, (p2 + 2) % 4], ag2_sem.at[c, h, 2])
            own = full.at[c, h, p1]
            hop(own, own, xy_send.at[c, 3], ag1_sem.at[c, h, 0], right)
            hop(own, own, xy_send.at[c, 3], ag1_sem.at[c, h, 1], left)

    def stage_forward1(c):
        for h in range(2):
            p1, right, left = first[h]
            for side, t, near in ((0, (p1 + 3) % 4, right), (1, (p1 + 1) % 4, left)):
                wait_bytes(full.at[c, h, t], ag1_sem.at[c, h, side])
                piece = full.at[c, h, t, :, side]
                hop(piece, piece, xy_send.at[c, 3], ag1_sem.at[c, h, 2], near)

    def stage_outputs(c):
        for h in range(2):
            wait_bytes(full.at[c, h, (first[h][0] + 2) % 4], ag1_sem.at[c, h, 2])
        out = jnp.zeros((rows, feat), F32)
        grad = jnp.zeros((rows, feat), F32)
        for b in range(4):
            cols = slice(b * col, (b + 1) * col)
            act, dgate, dup = (
                full[c, b // 2, :, :, b % 2, a].reshape(rows, col) for a in range(3)
            )
            out += dot(act, wd_ref[cols, :], ((1,), (0,)))
            grad += dot(dgate, wg_ref[:, cols], ((1,), (1,)))
            grad += dot(dup, wu_ref[:, cols], ((1,), (1,)))
        ret[c, :, 0:cap, :] = out.astype(BF16).reshape(blocks, cap, feat)
        ret[c, :, cap : 2 * cap, :] = grad.astype(BF16).reshape(blocks, cap, feat)

        def go(k):
            there = ((z + chunks * (k // 2) + c) % zs) * 2 + (core if k % 2 == 0 else 1 - core)
            pltpu.make_async_remote_copy(
                src_ref=ret.at[c, k],
                dst_ref=back.at[me],
                send_sem=back_send,
                recv_sem=back_recv,
                device_id=(dp, there),
                device_id_type=MESH,
            ).start()

        @pl.when(c == 0)
        def _():
            pltpu.make_async_copy(ret.at[c, 0], back.at[me], back_recv).start()

        @pl.when(c > 0)
        def _():
            go(0)

        for k in range(1, blocks):
            go(k)

        x = recv[c, :, 0:cap, :].reshape(rows, feat)
        g = recv[c, :, cap : 2 * cap, :].reshape(rows, feat)
        for b in range(4):
            cols = slice(b * col, (b + 1) * col)
            act, dgate, dup = (
                full[c, b // 2, :, :, b % 2, a].reshape(rows, col) for a in range(3)
            )
            acc_g[:, cols] += dot(x, dgate, ((0,), (0,)))
            acc_u[:, cols] += dot(x, dup, ((0,), (0,)))
            acc_d[cols, :] += dot(act, g, ((0,), (0,)))

    stages = (
        stage_partials,
        stage_relay1,
        stage_second,
        stage_relay2,
        stage_pointwise,
        stage_forward2,
        stage_first,
        stage_forward1,
        stage_outputs,
    )

    def step(u, carry):
        for r in range(LAG):
            for s in reversed(range(r, len(stages), LAG)):
                c = u - s // LAG

                @pl.when((c >= 0) & (c < chunks))
                def _(s=s, c=c):
                    stages[s](c)

        return carry

    lax.fori_loop(0, (len(stages) - 1) // LAG + chunks, step, 0)

    ggate_ref[...] = acc_g[...].astype(BF16)
    gup_ref[...] = acc_u[...].astype(BF16)
    gdown_ref[...] = acc_d[...].astype(BF16)

    wait_bytes(back, back_recv)
    sel = pick[...]
    token_out = dot(sel, back[:, 0:cap, :].reshape(slots, feat), ((1,), (0,)))
    mixed_ref[...] = (weight * token_out).astype(BF16)
    gtok_ref[...] = dot(
        sel, back[:, cap : 2 * cap, :].reshape(slots, feat), ((1,), (0,))
    ).astype(BF16)

    wait_bytes(send.at[0 : experts - 1], disp_send)
    wait_bytes(back.at[0 : experts - 1], back_send)
    for c in range(chunks):
        wait_bytes(part.at[c, 0:3], xy_send.at[c, 0])
        wait_bytes(red.at[c, 0:3], xy_send.at[c, 1])
        wait_bytes(full.at[c, :, 0, 0:3], xy_send.at[c, 2])
        wait_bytes(full.at[c, :, 0:3], xy_send.at[c, 3])


def body(tokens, grad_out, expert_ids, gates, w_gate, w_up, w_down):
    experts = lax.axis_size("expert")
    toks, feat = tokens.shape
    hid = w_gate.shape[-1]
    cap = toks // 16
    zs = experts // 2
    chunks = 4 if zs % 4 == 0 else zs
    rows = experts * cap // chunks
    q1, q2, col = rows // 4, rows // 16, hid // 4
    dma = pltpu.SemaphoreType.DMA
    results = pl.pallas_call(
        functools.partial(kernel, experts, cap, chunks),
        out_shape=(
            jax.ShapeDtypeStruct((toks, feat), BF16),
            jax.ShapeDtypeStruct((toks, feat), BF16),
            jax.ShapeDtypeStruct((feat, hid), BF16),
            jax.ShapeDtypeStruct((feat, hid), BF16),
            jax.ShapeDtypeStruct((hid, feat), BF16),
        ),
        in_specs=[pl.BlockSpec(memory_space=pltpu.VMEM)] * 7,
        out_specs=(pl.BlockSpec(memory_space=pltpu.VMEM),) * 5,
        scratch_shapes=[
            pltpu.VMEM((experts, 2 * cap, feat), BF16),
            pltpu.VMEM((chunks, experts // chunks, 2 * cap, feat), BF16),
            pltpu.VMEM((chunks, 4, 4, 3, q1, col), BF16),
            pltpu.VMEM((chunks, 2, 2, 3, q1, col), BF16),
            pltpu.VMEM((chunks, 2, 4, 3, q1, col), BF16),
            pltpu.VMEM((chunks, 4, 4, 3, q2, col), BF16),
            pltpu.VMEM((chunks, 2, 2, 3, q2, col), BF16),
            pltpu.VMEM((chunks, 2, 4, 3, q2, col), BF16),
            pltpu.VMEM((chunks, 2, 4, 4, 2, 3, q2, col), BF16),
            pltpu.VMEM((chunks, experts // chunks, 2 * cap, feat), BF16),
            pltpu.VMEM((experts, 2 * cap, feat), BF16),
            pltpu.VMEM((toks, experts * cap), BF16),
            pltpu.VMEM((feat, hid), F32),
            pltpu.VMEM((feat, hid), F32),
            pltpu.VMEM((hid, feat), F32),
            dma,
            dma((chunks,)),
            dma,
            dma,
            dma((chunks, 4)),
            dma((chunks, 2, 2)),
            dma((chunks, 2)),
            dma((chunks, 2, 2)),
            dma((chunks, 2)),
            dma((chunks, 2, 3)),
            dma((chunks, 2, 3)),
        ],
        compiler_params=pltpu.CompilerParams(
            collective_id=0, has_side_effects=True, vmem_limit_bytes=60 * 1024 * 1024
        ),
    )(tokens, grad_out, expert_ids, gates, w_gate[0], w_up[0], w_down[0])
    mixed, grad_tokens, grad_gate, grad_up, grad_down = results
    return (mixed, grad_tokens, grad_gate[None], grad_up[None], grad_down[None])


def solution(mesh):
    placed = (
        P("expert", "dp"),
        P("expert", "dp"),
        P("expert", None),
        P("expert", None),
        P("expert", "dp", None),
        P("expert", "dp", None),
        P("expert", None, "dp"),
    )
    return jax.shard_map(
        body,
        mesh=mesh,
        in_specs=placed,
        out_specs=(
            P("expert", "dp"),
            P("expert", "dp"),
            P("expert", "dp", None),
            P("expert", "dp", None),
            P("expert", None, "dp"),
        ),
        check_vma=False,
    )
```

time: 364 us -> 155 us (0.43)
  waiting for transfers between devices: 228 us -> 0 us
  Pallas kernels: 0 us -> 142 us
  blocking collectives: 50 us -> 0 us
  starting transfers between devices: 21.8 us -> 0 us
  matrix products: 16.2 us -> 0 us
  between operations: 14.3 us -> 0.67 us
  other arithmetic: 10.7 us -> 0 us
  local copies, waits for them, and re-layouts: 22 us -> 11.9 us
    psum x1 -> x0, waiting for transfers between devices: 145 us -> none  [body(): lax.psum(part_up.astype(jnp.bfloat16), 'dp').astype(jnp.float32)]
    pallas_call x0 -> x1, Pallas kernels: none -> 142 us  [body(): pl.pallas_call(functools.partial(kernel, experts, cap, chunks), out_shape...]
    all_to_all x3 -> x0, waiting for transfers between devices: 83.5 us -> none  [the longest x1 30 us: body(): lax.all_to_all(grad_blocks, 'expert', split_axis=0, concat_axis=0, tiled=...]
    all_to_all x1 -> x0, blocking collectives: 50 us -> none  [body(): lax.all_to_all(send_tokens, 'expert', split_axis=0, concat_axis=0, tiled=...]
    all_to_all x3 -> x0, starting transfers between devices: 21.7 us -> none  [the longest x1 13 us: body(): lax.all_to_all(grad_blocks, 'expert', split_axis=0, concat_axis=0, tiled=...]
    dot_general x9 -> x0, matrix products: 16.2 us -> none  [the longest x3 6.13 us: contract_rows(): lax.dot_general(left, right, (((0,), (0,)), ((), ())), preferred_element_...]
    gather x4 -> x0, local copies, waits for them, and re-layouts: 12.5 us -> none  [the longest x1 3.94 us: body(): jnp.take(scaled, source_row, axis=0, mode='fill', fill_value=0)]
    unnamed x22 -> x24, local copies, waits for them, and re-layouts: 4.81 us -> 11.9 us
  transfers between devices with their start and end apart: 4 -> 0, of which waited for: 4 -> 0; matrix products, arithmetic and copies ran while one was open for 5% -> 0% of each run, Pallas kernels for 0% -> 0%
where the time goes in v1:
time: 155 us
  Pallas kernels  142 us (92%)
  local copies, waits for them, and re-layouts  11.9 us (8%)
    pallas_call x1, Pallas kernels, body(): pl.pallas_call(functools.partial(kernel, experts, cap, chunks), out_shape...  142 us
    unnamed x24, local copies, waits for them, and re-layouts  11.9 us

profile of v1, /device:TPU:1, one launch (start us, length us, event | category | flops | bytes accessed | tf_op | source)
XLA Modules:
  0.0 154.8 jit_solution(13032706067893197773)
XLA Ops:
  0.6 0.0 copy-start.4
  0.6 1.8 %copy.13.tok_ref = bf16[512,224]{1,0:T(8,128)(2,1)} copy(bf16[512,224]{0,1:T(8,128)(2,1)} %param.7) | data formatting | bytes 458752 | tf_op args[0]
  2.5 0.0 copy-done.4
  2.5 0.0 copy-start.5
  2.5 0.0 copy-start.3
  2.5 0.8 copy.14.gout_ref
  3.3 0.0 copy-done.5
  3.3 0.0 copy-start.6
  3.3 0.8 copy.15.ids_ref
  4.2 0.0 copy-done.6
  4.2 0.9 copy.16.gates_ref
  5.0 0.0 copy-done.3
  5.0 1.0 copy.12
  6.0 142.2 %shard_map.110 = (bf16[512,224]{1,0:T(8,128)(2,1)}, bf16[512,224]{1,0:T(8,128)(2,1)}, bf16[224,1024]{1,0:T(8,128)(2,1)}, bf16[224,1024]{1,0:T(8,128)(2,1)}, bf16[1024,224]{1,0:T(8,128)(2,1)}) custom-call(bf16[512,224]{1,0:T(8,128)(2,1)} %copy.13.tok_ref, bf16[512,224]{1,0:T(8,128)(2,1)} %copy.14.gout_ref, s32[512,8]{1,0:T(8,128)} %copy.15.ids_ref, ...), custom_call_target="tpu_custom_call" | custom-call | tf_op jit(solution)/shard_map/pallas_call | solution.py:369
  148.2 0.0 copy-start
  148.2 1.8 %copy.17 = bf16[512,224]{0,1:T(8,128)(2,1)} copy(bf16[512,224]{1,0:T(8,128)(2,1)} %get-tuple-element.15) | data formatting | bytes 458752
  150.1 1.8 %copy.18 = bf16[512,224]{0,1:T(8,128)(2,1)} copy(bf16[512,224]{1,0:T(8,128)(2,1)} %get-tuple-element.16) | data formatting | bytes 458752
  151.8 0.0 copy-done
  151.8 0.0 copy-start.2
  151.9 1.0 copy.19
  152.8 0.0 copy-done.2
  152.9 0.0 copy-start.1
  152.9 0.8 copy.22
  153.6 0.4 copy-done.1
  154.1 0.8 copy.23
Async XLA Ops:
  0.6 1.8 %copy-start.4 = (bf16[512,224]{0,1:T(8,128)(2,1)S(1)}, bf16[512,224]{0,1:T(8,128)(2,1)}, u32[]{:S(2)}) copy-start(bf16[512,224]{0,1:T(8,128)(2,1)} %param.8) | copy-start | bytes 688132
  2.5 0.8 copy-start.5
  2.5 2.5 %copy-start.3 = (bf16[1,1024,224]{1,2,0:T(8,128)(2,1)S(1)}, bf16[1,1024,224]{1,2,0:T(8,128)(2,1)}, u32[]{:S(2)}) copy-start(bf16[1,1024,224]{1,2,0:T(8,128)(2,1)} %param.13) | copy-start | bytes 1376260
  3.3 0.8 copy-start.6
  148.2 3.6 %copy-start = (bf16[1024,224]{1,0:T(8,128)(2,1)S(1)}, bf16[1024,224]{1,0:T(8,128)(2,1)}, u32[]{:S(2)}) copy-start(bf16[1024,224]{1,0:T(8,128)(2,1)} %get-tuple-element.14) | copy-start | bytes 1376260
  151.8 1.0 copy-start.2
  152.9 1.2 copy-start.1

commit v2 on v1

v2 whole, which is shorter than its diff:
```python
import functools

import jax
import jax.numpy as jnp
from jax import lax
from jax.experimental import pallas as pl
from jax.experimental.pallas import tpu as pltpu
from jax.sharding import PartitionSpec as P

MESH = pl.DeviceIdType.MESH
BF16 = jnp.bfloat16
F32 = jnp.float32
RING = 4
STARTS = (0, 1, 4, 5, 7, 8, 11, 12)
LANES = 128


def dot(left, right, dims):
    return lax.dot_general(left, right, (dims, ((), ())), preferred_element_type=F32)


def z_wait(ref, sem):
    pltpu.make_async_copy(ref, ref, sem).wait()


def xy_wait(ref, sem):
    pltpu.make_async_copy(ref, ref, sem).wait()


def z_send(src, dst, send_sem, recv_sem, device):
    pltpu.make_async_remote_copy(src, dst, send_sem, recv_sem, device, MESH).start()


def xy_send_to(src, dst, send_sem, recv_sem, device):
    pltpu.make_async_remote_copy(src, dst, send_sem, recv_sem, device, MESH).start()


def kernel(
    experts,
    cap,
    chunks,
    tok_ref,
    gout_ref,
    ids_ref,
    gates_ref,
    wg_ref,
    wu_ref,
    wd_ref,
    mixed_ref,
    gtok_ref,
    ggate_ref,
    gup_ref,
    gdown_ref,
    send,
    recv,
    part,
    ra1,
    rb1,
    red,
    ra2,
    rb2,
    full,
    ret,
    back,
    place,
    comb,
    wgp,
    wup,
    wdp,
    xs,
    gs,
    acc_g,
    acc_u,
    acc_d,
    disp_send,
    disp_recv,
    back_send,
    back_recv,
    xy_send,
    ra1_sem,
    rb1_sem,
    ra2_sem,
    rb2_sem,
    ag2_sem,
    ag1_sem,
):
    dp = lax.axis_index("dp")
    me = lax.axis_index("expert")
    px, py = dp // RING, dp % RING
    zs = experts // 2
    z, core = me // 2, me % 2
    per = zs // chunks
    blocks = 2 * per
    rows = blocks * cap
    feat, toks = tok_ref.shape
    slots = experts * cap
    col = part.shape[-1]
    q2 = red.shape[-2]

    def peer(dz, dc):
        return ((z + dz) % zs) * 2 + (core if dc == 0 else 1 - core)

    def x_peer(step):
        return ((px + step) % RING) * RING + py

    def y_peer(step):
        return px * RING + (py + step) % RING

    def distance(c, j):
        base = per * c
        if chunks == len(STARTS):
            late = c // (chunks // 2)
            base = 2 * per * ((1 - late) * c + late * (chunks - 1 - c)) + late * per
        k = base + j
        far, odd = (k + 1) // 2, k % 2
        return (odd * far + (1 - odd) * (zs - far)) % zs

    barrier = pltpu.get_barrier_semaphore()
    for dz in range(zs):
        for dc in range(2):
            if dz or dc:
                pl.semaphore_signal(
                    barrier, inc=1, device_id=(dp, peer(dz, dc)), device_id_type=MESH
                )
    for near in (x_peer(1), x_peer(RING - 1), y_peer(1), y_peer(RING - 1)):
        pl.semaphore_signal(barrier, inc=1, device_id=(near, me), device_id_type=MESH)

    ids = ids_ref[...]
    inside = ids < experts
    chosen = jnp.sum(jnp.where(inside, ids, 0).astype(F32), axis=0, keepdims=True)
    routed = jnp.sum(jnp.where(inside, 1.0, 0.0), axis=0, keepdims=True)
    weight = jnp.sum(jnp.where(inside, gates_ref[...], 0.0), axis=0, keepdims=True)
    row_e = lax.broadcasted_iota(jnp.int32, (experts, toks), 0).astype(F32)
    one_hot = jnp.where((row_e == chosen) & (routed > 0.0), 1.0, 0.0)
    earlier = jnp.where(
        lax.broadcasted_iota(jnp.int32, (toks, toks), 0)
        < lax.broadcasted_iota(jnp.int32, (toks, toks), 1),
        1.0,
        0.0,
    ).astype(BF16)
    counts = dot(one_hot.astype(BF16), earlier, ((1,), (0,)))
    position = jnp.sum(counts * one_hot, axis=0, keepdims=True)
    slot = jnp.where(routed > 0.0, chosen * cap + position, 2.0 * slots)
    row_s = lax.broadcasted_iota(jnp.int32, (slots, toks), 0).astype(F32)
    place[...] = jnp.where(row_s == slot, 1.0, 0.0).astype(BF16)
    scaled = (weight * gout_ref[...].astype(F32)).astype(BF16)
    wide = feat - LANES
    cut = 2 * LANES - wide
    comb[0:LANES, :] = tok_ref[0:LANES, :]
    comb[LANES : 2 * LANES, :] = scaled[0:LANES, :]
    comb[2 * LANES : 2 * LANES + wide, :] = tok_ref[LANES:feat, :]
    comb[2 * LANES + wide : 3 * LANES, :] = scaled[LANES:cut, :]
    comb[3 * LANES : 3 * LANES + feat - cut, :] = scaled[cut:feat, :]
    comb[3 * LANES + feat - cut : 4 * LANES, :] = scaled[cut:feat, :]
    laid = dot(place[...], comb[...], ((1,), (1,)))
    for i in range(3):
        send[:, i * cap : (i + 1) * cap, :] = (
            laid[:, i * LANES : (i + 1) * LANES].astype(BF16).reshape(experts, cap, LANES)
        )
    last = laid[:, 3 * LANES : 4 * LANES].reshape(experts, cap, LANES)
    half = cap // 2
    lane = lax.broadcasted_iota(jnp.int32, (1, 1, LANES), 2)
    send[:, 3 * cap : 3 * cap + half, :] = jnp.where(
        lane < LANES // 2, last[:, 0:half, :], last[:, half:cap, :]
    ).astype(BF16)

    pl.semaphore_wait(barrier, 2 * zs - 1 + 4)

    for c in range(chunks):
        for j in range(per):
            for dc in range(2):
                dz = distance(c, j)
                target = recv.at[c, 2 * j + dc]
                if dz == 0 and dc == 0:
                    pltpu.make_async_copy(send.at[me], target, disp_recv.at[c]).start()
                else:
                    there = peer(zs - dz, dc)
                    z_send(send.at[there], target, disp_send, disp_recv.at[c], (dp, there))

    none = jnp.zeros((2 * LANES - feat, wg_ref.shape[1]), BF16)
    for padded, ref in ((wgp, wg_ref), (wup, wu_ref)):
        padded[0:feat, :] = ref[...]
        padded[feat : 2 * LANES, :] = none
    wdp[0:LANES, :] = wd_ref[0:LANES, :]
    wdp[LANES : LANES + feat - cut, :] = wd_ref[cut:feat, :]
    wdp[LANES + feat - cut : LANES + wide, :] = none
    wdp[LANES + wide : 2 * LANES, :] = wd_ref[LANES:cut, :]

    def unpack(rows3, count):
        first_x = rows3[:, 0:cap, :]
        first_g = rows3[:, cap : 2 * cap, :]
        both = rows3[:, 2 * cap : 3 * cap, :]
        pair = rows3[:, 3 * cap : 3 * cap + half, :].astype(F32)
        other = pltpu.roll(pair.reshape(count * half, LANES), LANES // 2, 1)
        pair = jnp.concatenate([pair, other.reshape(count, half, LANES)], axis=1)
        rest = jnp.where(
            lane < LANES // 2, pair, jnp.where(lane >= wide, both.astype(F32), 0.0)
        ).astype(BF16)
        n = count * cap
        return (
            (first_x.reshape(n, LANES), both.reshape(n, LANES)),
            (first_g.reshape(n, LANES), rest.reshape(n, LANES)),
        )

    acc_g[...] = jnp.zeros_like(acc_g)
    acc_u[...] = jnp.zeros_like(acc_u)
    acc_d[...] = jnp.zeros_like(acc_d)

    def hop(src, dst, send_sem, recv_sem, near):
        xy_send_to(src, dst, send_sem, recv_sem, (near, me))

    first = ((px, x_peer(1), x_peer(RING - 1)), (py, y_peer(1), y_peer(RING - 1)))
    second = (first[1], first[0])

    def rs_start(src, ra, rb, c, h, ring, ssem, ra_sem, rb_sem):
        p, right, left = ring
        lo, hi = 2 * h, 2 * h + 1
        hop(src.at[c, lo, (p + 2) % 4], ra.at[c, h, 0], ssem, ra_sem.at[c, h, 0], right)
        hop(src.at[c, hi, (p + 2) % 4], ra.at[c, h, 1], ssem, ra_sem.at[c, h, 1], left)
        hop(src.at[c, hi, (p + 1) % 4], rb.at[c, h, 0], ssem, rb_sem.at[c, h], right)
        hop(src.at[c, lo, (p + 3) % 4], rb.at[c, h, 1], ssem, rb_sem.at[c, h], left)

    def rs_relay(src, ra, rb, c, h, ring, ssem, ra_sem, rb_sem):
        p, right, left = ring
        for side, b, t, near in ((0, 2 * h, (p + 1) % 4, right), (1, 2 * h + 1, (p + 3) % 4, left)):
            xy_wait(ra.at[c, h, side], ra_sem.at[c, h, side])
            src[c, b, t] = (src[c, b, t].astype(F32) + ra[c, h, side].astype(F32)).astype(BF16)
            hop(src.at[c, b, t], rb.at[c, h, 2 + side], ssem, rb_sem.at[c, h], near)

    def rs_final(src, rb, c, h, ring, rb_sem):
        p = ring[0]
        xy_wait(rb.at[c, h], rb_sem.at[c, h])
        lo = src[c, 2 * h, p].astype(F32) + rb[c, h, 1].astype(F32) + rb[c, h, 2].astype(F32)
        hi = src[c, 2 * h + 1, p].astype(F32) + rb[c, h, 0].astype(F32) + rb[c, h, 3].astype(F32)
        return lo, hi

    def stage_partials(c):
        z_wait(recv.at[c], disp_recv.at[c])
        x_pair, g_pair = unpack(recv[c], blocks)
        for i in range(2):
            xs[c, :, i * LANES : (i + 1) * LANES] = x_pair[i]
            gs[c, :, i * LANES : (i + 1) * LANES] = g_pair[i]
        x = xs[c]
        g = gs[c]
        for h in range(2):
            for b in (2 * h, 2 * h + 1):
                cols = slice(b * col, (b + 1) * col)
                terms = (
                    dot(x, wgp[:, cols], ((1,), (0,))),
                    dot(x, wup[:, cols], ((1,), (0,))),
                    dot(g, wdp[:, cols], ((1,), (0,))),
                )
                for a in range(3):
                    part[c, b, :, a] = terms[a].astype(BF16).reshape(4, rows // 4, col)
            rs_start(part, ra1, rb1, c, h, first[h], xy_send.at[c, 0], ra1_sem, rb1_sem)

    def stage_relay1(c):
        for h in range(2):
            rs_relay(part, ra1, rb1, c, h, first[h], xy_send.at[c, 0], ra1_sem, rb1_sem)

    def stage_second(c):
        for h in range(2):
            sums = rs_final(part, rb1, c, h, first[h], rb1_sem)
            for side in range(2):
                for a in range(3):
                    red[c, 2 * h + side, :, a] = sums[side][a].astype(BF16).reshape(4, q2, col)
            rs_start(red, ra2, rb2, c, h, second[h], xy_send.at[c, 1], ra2_sem, rb2_sem)

    def stage_relay2(c):
        for h in range(2):
            rs_relay(red, ra2, rb2, c, h, second[h], xy_send.at[c, 1], ra2_sem, rb2_sem)

    def stage_pointwise(c):
        for h in range(2):
            p1 = first[h][0]
            p2, right, left = second[h]
            sums = rs_final(red, rb2, c, h, second[h], rb2_sem)
            for side in range(2):
                gate, up, grad = sums[side][0], sums[side][1], sums[side][2]
                logistic = 1.0 / (1.0 + jnp.exp(-gate))
                swish = gate * logistic
                full[c, h, p1, p2, side, 0] = (swish * up).astype(BF16)
                full[c, h, p1, p2, side, 1] = (
                    grad * up * (logistic * (1.0 + gate * (1.0 - logistic)))
                ).astype(BF16)
                full[c, h, p1, p2, side, 2] = (grad * swish).astype(BF16)
            own = full.at[c, h, p1, p2]
            hop(own, own, xy_send.at[c, 2], ag2_sem.at[c, h, 0], right)
            hop(own, own, xy_send.at[c, 2], ag2_sem.at[c, h, 1], left)

    def stage_forward2(c):
        for h in range(2):
            p1 = first[h][0]
            p2, right, left = second[h]
            for side, t, near in ((0, (p2 + 3) % 4, right), (1, (p2 + 1) % 4, left)):
                xy_wait(full.at[c, h, p1, t], ag2_sem.at[c, h, side])
                piece = full.at[c, h, p1, t, side]
                hop(piece, piece, xy_send.at[c, 2], ag2_sem.at[c, h, 2], near)

    def stage_first(c):
        for h in range(2):
            p1, right, left = first[h]
            p2 = second[h][0]
            xy_wait(full.at[c, h, p1, (p2 + 2) % 4], ag2_sem.at[c, h, 2])
            own = full.at[c, h, p1]
            hop(own, own, xy_send.at[c, 3], ag1_sem.at[c, h, 0], right)
            hop(own, own, xy_send.at[c, 3], ag1_sem.at[c, h, 1], left)

    def stage_forward1(c):
        for h in range(2):
            p1, right, left = first[h]
            for side, t, near in ((0, (p1 + 3) % 4, right), (1, (p1 + 1) % 4, left)):
                xy_wait(full.at[c, h, t], ag1_sem.at[c, h, side])
                piece = full.at[c, h, t, :, side]
                hop(piece, piece, xy_send.at[c, 3], ag1_sem.at[c, h, 2], near)

    def stage_outputs(c):
        for h in range(2):
            xy_wait(full.at[c, h, (first[h][0] + 2) % 4], ag1_sem.at[c, h, 2])
        out = jnp.zeros((rows, 2 * LANES), F32)
        grad = jnp.zeros((rows, 2 * LANES), F32)
        for b in range(4):
            cols = slice(b * col, (b + 1) * col)
            act, dgate, dup = (
                full[c, b // 2, :, :, b % 2, a].reshape(rows, col) for a in range(3)
            )
            out += dot(act, wdp[:, cols], ((1,), (1,)))
            grad += dot(dgate, wgp[:, cols], ((1,), (1,)))
            grad += dot(dup, wup[:, cols], ((1,), (1,)))
        packed = (blocks, cap, LANES)
        rest = out[:, LANES : 2 * LANES].reshape(packed)
        turned = pltpu.roll(rest[:, half:cap, :].reshape(blocks * half, LANES), LANES // 2, 1)
        ret[c, :, 0:cap, :] = grad[:, 0:LANES].astype(BF16).reshape(packed)
        ret[c, :, cap : 2 * cap, :] = out[:, 0:LANES].astype(BF16).reshape(packed)
        ret[c, :, 2 * cap : 3 * cap, :] = jnp.where(
            lane < wide, grad[:, LANES : 2 * LANES].reshape(packed), rest
        ).astype(BF16)
        ret[c, :, 3 * cap : 3 * cap + half, :] = jnp.where(
            lane < LANES // 2, rest[:, 0:half, :], turned.reshape(blocks, half, LANES)
        ).astype(BF16)

        def go(k):
            there = peer(distance(c, k // 2), k % 2)
            z_send(ret.at[c, k], back.at[me], back_send, back_recv, (dp, there))

        @pl.when(c == 0)
        def _():
            pltpu.make_async_copy(ret.at[c, 0], back.at[me], back_recv).start()

        @pl.when(c > 0)
        def _():
            go(0)

        for k in range(1, blocks):
            go(k)

        x = xs[c]
        g = gs[c]
        for b in range(4):
            cols = slice(b * col, (b + 1) * col)
            act, dgate, dup = (
                full[c, b // 2, :, :, b % 2, a].reshape(rows, col) for a in range(3)
            )
            acc_g[:, cols] += dot(x, dgate, ((0,), (0,)))
            acc_u[:, cols] += dot(x, dup, ((0,), (0,)))
            acc_d[:, cols] += dot(g, act, ((0,), (0,)))

    stages = (
        stage_partials,
        stage_relay1,
        stage_second,
        stage_relay2,
        stage_pointwise,
        stage_forward2,
        stage_first,
        stage_forward1,
        stage_outputs,
    )

    starts = STARTS[:chunks]

    def step(t, carry):
        for s in reversed(range(len(stages))):
            since = t - s
            c = sum((since >= begin).astype(jnp.int32) for begin in starts[1:])

            @pl.when(functools.reduce(jnp.logical_or, [since == begin for begin in starts]))
            def _(s=s, c=c):
                stages[s](c)

        return carry

    lax.fori_loop(0, len(stages) + starts[-1], step, 0)

    def restore(ref, value):
        ref[0:LANES, :] = value[0:LANES].astype(BF16)
        ref[LANES:cut, :] = value[LANES + wide : 2 * LANES].astype(BF16)
        ref[cut:feat, :] = value[LANES : LANES + feat - cut].astype(BF16)

    ggate_ref[...] = acc_g[0:feat, :].astype(BF16)
    gup_ref[...] = acc_u[0:feat, :].astype(BF16)
    restore(gdown_ref, acc_d[...])

    z_wait(back, back_recv)
    grad_pair, out_pair = unpack(back[...], experts)
    spots = ((0,), (0,))
    restore(mixed_ref, weight * dot(jnp.concatenate(out_pair, axis=1), place[...], spots))
    gtok_ref[...] = dot(jnp.concatenate(grad_pair, axis=1), place[...], spots)[0:feat].astype(BF16)

    z_wait(send.at[0 : experts - 1], disp_send)
    z_wait(back.at[0 : experts - 1], back_send)
    for c in range(chunks):
        xy_wait(part.at[c, 0:3], xy_send.at[c, 0])
        xy_wait(red.at[c, 0:3], xy_send.at[c, 1])
        xy_wait(full.at[c, :, 0, 0:3], xy_send.at[c, 2])
        xy_wait(full.at[c, :, 0:3], xy_send.at[c, 3])


def body(tokens, grad_out, expert_ids, gates, w_gate, w_up, w_down):
    experts = lax.axis_size("expert")
    toks, feat = tokens.shape
    hid = w_gate.shape[-1]
    cap = toks // 16
    zs = experts // 2
    chunks = min(len(STARTS), zs)
    rows = experts * cap // chunks
    q1, q2, col = rows // 4, rows // 16, hid // 4
    packed = 3 * cap + cap // 2
    dma = pltpu.SemaphoreType.DMA
    results = pl.pallas_call(
        functools.partial(kernel, experts, cap, chunks),
        out_shape=(
            jax.ShapeDtypeStruct((feat, toks), BF16),
            jax.ShapeDtypeStruct((feat, toks), BF16),
            jax.ShapeDtypeStruct((feat, hid), BF16),
            jax.ShapeDtypeStruct((feat, hid), BF16),
            jax.ShapeDtypeStruct((feat, hid), BF16),
        ),
        in_specs=[pl.BlockSpec(memory_space=pltpu.VMEM)] * 7,
        out_specs=(pl.BlockSpec(memory_space=pltpu.VMEM),) * 5,
        scratch_shapes=[
            pltpu.VMEM((experts, packed, LANES), BF16),
            pltpu.VMEM((chunks, experts // chunks, packed, LANES), BF16),
            pltpu.VMEM((chunks, 4, 4, 3, q1, col), BF16),
            pltpu.VMEM((chunks, 2, 2, 3, q1, col), BF16),
            pltpu.VMEM((chunks, 2, 4, 3, q1, col), BF16),
            pltpu.VMEM((chunks, 4, 4, 3, q2, col), BF16),
            pltpu.VMEM((chunks, 2, 2, 3, q2, col), BF16),
            pltpu.VMEM((chunks, 2, 4, 3, q2, col), BF16),
            pltpu.VMEM((chunks, 2, 4, 4, 2, 3, q2, col), BF16),
            pltpu.VMEM((chunks, experts // chunks, packed, LANES), BF16),
            pltpu.VMEM((experts, packed, LANES), BF16),
            pltpu.VMEM((experts * cap, toks), BF16),
            pltpu.VMEM((4 * LANES, toks), BF16),
            pltpu.VMEM((2 * LANES, hid), BF16),
            pltpu.VMEM((2 * LANES, hid), BF16),
            pltpu.VMEM((2 * LANES, hid), BF16),
            pltpu.VMEM((chunks, rows, 2 * LANES), BF16),
            pltpu.VMEM((chunks, rows, 2 * LANES), BF16),
            pltpu.VMEM((2 * LANES, hid), F32),
            pltpu.VMEM((2 * LANES, hid), F32),
            pltpu.VMEM((2 * LANES, hid), F32),
            dma,
            dma((chunks,)),
            dma,
            dma,
            dma((chunks, 4)),
            dma((chunks, 2, 2)),
            dma((chunks, 2)),
            dma((chunks, 2, 2)),
            dma((chunks, 2)),
            dma((chunks, 2, 3)),
            dma((chunks, 2, 3)),
        ],
        compiler_params=pltpu.CompilerParams(
            collective_id=0, has_side_effects=True, vmem_limit_bytes=60 * 1024 * 1024
        ),
    )(tokens.T, grad_out.T, expert_ids.T, gates.T, w_gate[0], w_up[0], w_down[0].T)
    mixed, grad_tokens, grad_gate, grad_up, grad_down = results
    return (mixed.T, grad_tokens.T, grad_gate[None], grad_up[None], grad_down.T[None])


def solution(mesh):
    placed = (
        P("expert", "dp"),
        P("expert", "dp"),
        P("expert", None),
        P("expert", None),
        P("expert", "dp", None),
        P("expert", "dp", None),
        P("expert", None, "dp"),
    )
    return jax.shard_map(
        body,
        mesh=mesh,
        in_specs=placed,
        out_specs=(
            P("expert", "dp"),
            P("expert", "dp"),
            P("expert", "dp", None),
            P("expert", "dp", None),
            P("expert", None, "dp"),
        ),
        check_vma=False,
    )
```

time: 155 us -> 132 us (0.85)
  Pallas kernels: 142 us -> 126 us
  local copies, waits for them, and re-layouts: 11.9 us -> 5.54 us
    pallas_call x1, Pallas kernels: 142 us -> 126 us  [body(): pl.pallas_call(functools.partial(kernel, experts, cap, chunks), out_shape...]
    unnamed x24 -> x13, local copies, waits for them, and re-layouts: 11.9 us -> 5.54 us
where the time goes in v2:
time: 132 us
  Pallas kernels  126 us (95%)
  local copies, waits for them, and re-layouts  5.54 us (4%)
    pallas_call x1, Pallas kernels, body(): pl.pallas_call(functools.partial(kernel, experts, cap, chunks), out_shape...  126 us
    unnamed x13, local copies, waits for them, and re-layouts  5.54 us

profile of v2, /device:TPU:1, one launch (start us, length us, event | category | flops | bytes accessed | tf_op | source)
XLA Modules:
  0.0 131.8 jit_solution(14028869854812446910)
XLA Ops:
  0.6 125.6 %shard_map.110 = (bf16[224,512]{1,0:T(8,128)(2,1)}, bf16[224,512]{1,0:T(8,128)(2,1)}, bf16[224,1024]{1,0:T(8,128)(2,1)}, bf16[224,1024]{1,0:T(8,128)(2,1)}, bf16[224,1024]{1,0:T(8,128)(2,1)}) custom-call(bf16[224,512]{1,0:T(8,128)(2,1)} %bitcast.22, bf16[224,512]{1,0:T(8,128)(2,1)} %bitcast.23, s32[8,512]{1,0:T(8,128)} %bitcast.26, f32[8,512]{1,0:T(8,128)} %bitcast.27, ...), custom_call_target="tpu_custom_call" | custom-call | tf_op jit(solution)/shard_map/pallas_call | solution.py:430
  126.2 0.0 copy-start.3
  126.3 0.0 copy-start.2
  126.3 1.7 %copy.17 = bf16[512,224]{0,1:T(8,128)(2,1)} copy(bf16[512,224]{0,1:T(8,128)(2,1)} %bitcast.25) | data formatting | bytes 458752
  128.0 0.0 copy-done.3
  128.0 0.7 copy.18
  128.7 0.0 copy-done.2
  128.7 0.0 copy-start.1
  128.7 0.8 copy.19
  129.4 0.4 copy-done.1
  129.8 0.0 copy-start
  129.8 0.8 copy.20
  130.6 0.4 copy-done
  131.0 0.8 copy.21
Async XLA Ops:
  126.2 1.7 %copy-start.3 = (bf16[224,512]{1,0:T(8,128)(2,1)S(1)}, bf16[224,512]{1,0:T(8,128)(2,1)}, u32[]{:S(2)}) copy-start(bf16[224,512]{1,0:T(8,128)(2,1)} %get-tuple-element.11) | copy-start | bytes 688132
  126.3 2.4 %copy-start.2 = (bf16[224,1024]{1,0:T(8,128)(2,1)S(1)}, bf16[224,1024]{1,0:T(8,128)(2,1)}, u32[]{:S(2)}) copy-start(bf16[224,1024]{1,0:T(8,128)(2,1)} %get-tuple-element.12) | copy-start | bytes 1376260
  128.7 1.2 copy-start.1
  129.8 1.2 copy-start

commit v3 on v2

--- a/solution.py
+++ b/solution.py
@@ -69,9 +69,13 @@
     wdp,
     xs,
     gs,
-    acc_g,
-    acc_u,
-    acc_d,
+    out_m,
+    out_t,
+    out_g,
+    out_u,
+    out_d,
+    in_sem,
+    out_sem,
     disp_send,
     disp_recv,
     back_send,
@@ -125,6 +129,22 @@
     for near in (x_peer(1), x_peer(RING - 1), y_peer(1), y_peer(RING - 1)):
         pl.semaphore_signal(barrier, inc=1, device_id=(near, me), device_id_type=MESH)
 
+    wide = feat - LANES
+    cut = 2 * LANES - wide
+    pieces = (
+        (wg_ref, wgp.at[0:feat]),
+        (wu_ref, wup.at[0:feat]),
+        (wd_ref.at[0:LANES], wdp.at[0:LANES]),
+        (wd_ref.at[cut:feat], wdp.at[LANES : LANES + feat - cut]),
+        (wd_ref.at[LANES:cut], wdp.at[LANES + wide : 2 * LANES]),
+    )
+    loads = [pltpu.make_async_copy(pair[0], pair[1], in_sem.at[i]) for i, pair in enumerate(pieces)]
+    for load in loads:
+        load.start()
+    wgp[feat : 2 * LANES, :] = jnp.zeros((2 * LANES - feat, wgp.shape[1]), BF16)
+    wup[feat : 2 * LANES, :] = jnp.zeros((2 * LANES - feat, wgp.shape[1]), BF16)
+    wdp[LANES + feat - cut : LANES + wide, :] = jnp.zeros((wide + cut - feat, wgp.shape[1]), BF16)
+
     ids = ids_ref[...]
     inside = ids < experts
     chosen = jnp.sum(jnp.where(inside, ids, 0).astype(F32), axis=0, keepdims=True)
@@ -144,8 +164,6 @@
     row_s = lax.broadcasted_iota(jnp.int32, (slots, toks), 0).astype(F32)
     place[...] = jnp.where(row_s == slot, 1.0, 0.0).astype(BF16)
     scaled = (weight * gout_ref[...].astype(F32)).astype(BF16)
-    wide = feat - LANES
-    cut = 2 * LANES - wide
     comb[0:LANES, :] = tok_ref[0:LANES, :]
     comb[LANES : 2 * LANES, :] = scaled[0:LANES, :]
     comb[2 * LANES : 2 * LANES + wide, :] = tok_ref[LANES:feat, :]
@@ -177,15 +195,6 @@
                     there = peer(zs - dz, dc)
                     z_send(send.at[there], target, disp_send, disp_recv.at[c], (dp, there))
 
-    none = jnp.zeros((2 * LANES - feat, wg_ref.shape[1]), BF16)
-    for padded, ref in ((wgp, wg_ref), (wup, wu_ref)):
-        padded[0:feat, :] = ref[...]
-        padded[feat : 2 * LANES, :] = none
-    wdp[0:LANES, :] = wd_ref[0:LANES, :]
-    wdp[LANES : LANES + feat - cut, :] = wd_ref[cut:feat, :]
-    wdp[LANES + feat - cut : LANES + wide, :] = none
-    wdp[LANES + wide : 2 * LANES, :] = wd_ref[LANES:cut, :]
-
     def unpack(rows3, count):
         first_x = rows3[:, 0:cap, :]
         first_g = rows3[:, cap : 2 * cap, :]
@@ -202,9 +211,8 @@
             (first_g.reshape(n, LANES), rest.reshape(n, LANES)),
         )
 
-    acc_g[...] = jnp.zeros_like(acc_g)
-    acc_u[...] = jnp.zeros_like(acc_u)
-    acc_d[...] = jnp.zeros_like(acc_d)
+    for load in loads:
+        load.wait()
 
     def hop(src, dst, send_sem, recv_sem, near):
         xy_send_to(src, dst, send_sem, recv_sem, (near, me))
@@ -354,17 +362,6 @@
         for k in range(1, blocks):
             go(k)
 
-        x = xs[c]
-        g = gs[c]
-        for b in range(4):
-            cols = slice(b * col, (b + 1) * col)
-            act, dgate, dup = (
-                full[c, b // 2, :, :, b % 2, a].reshape(rows, col) for a in range(3)
-            )
-            acc_g[:, cols] += dot(x, dgate, ((0,), (0,)))
-            acc_u[:, cols] += dot(x, dup, ((0,), (0,)))
-            acc_d[:, cols] += dot(g, act, ((0,), (0,)))
-
     stages = (
         stage_partials,
         stage_relay1,
@@ -397,15 +394,31 @@
         ref[LANES:cut, :] = value[LANES + wide : 2 * LANES].astype(BF16)
         ref[cut:feat, :] = value[LANES : LANES + feat - cut].astype(BF16)
 
-    ggate_ref[...] = acc_g[0:feat, :].astype(BF16)
-    gup_ref[...] = acc_u[0:feat, :].astype(BF16)
-    restore(gdown_ref, acc_d[...])
+    x_t = xs[...].reshape(slots, 2 * LANES).T
+    g_t = gs[...].reshape(slots, 2 * LANES).T
+    for b in range(4):
+        cols = slice(b * col, (b + 1) * col)
+        act, dgate, dup = (
+            full[:, b // 2, :, :, b % 2, a].reshape(slots, col) for a in range(3)
+        )
+        out_g[:, cols] = dot(x_t, dgate, ((1,), (0,)))[0:feat].astype(BF16)
+        out_u[:, cols] = dot(x_t, dup, ((1,), (0,)))[0:feat].astype(BF16)
+        restore(out_d.at[:, cols], dot(g_t, act, ((1,), (0,))))
+
+    def leave(i, src, dst):
+        out = pltpu.make_async_copy(src, dst, out_sem.at[i])
+        out.start()
+        return out
+
+    outs = [leave(0, out_g, ggate_ref), leave(1, out_u, gup_ref), leave(2, out_d, gdown_ref)]
 
     z_wait(back, back_recv)
     grad_pair, out_pair = unpack(back[...], experts)
     spots = ((0,), (0,))
-    restore(mixed_ref, weight * dot(jnp.concatenate(out_pair, axis=1), place[...], spots))
-    gtok_ref[...] = dot(jnp.concatenate(grad_pair, axis=1), place[...], spots)[0:feat].astype(BF16)
+    restore(out_m, weight * dot(jnp.concatenate(out_pair, axis=1), place[...], spots))
+    outs.append(leave(3, out_m, mixed_ref))
+    out_t[...] = dot(jnp.concatenate(grad_pair, axis=1), place[...], spots)[0:feat].astype(BF16)
+    outs.append(leave(4, out_t, gtok_ref))
 
     z_wait(send.at[0 : experts - 1], disp_send)
     z_wait(back.at[0 : experts - 1], back_send)
@@ -414,6 +427,22 @@
         xy_wait(red.at[c, 0:3], xy_send.at[c, 1])
         xy_wait(full.at[c, :, 0, 0:3], xy_send.at[c, 2])
         xy_wait(full.at[c, :, 0:3], xy_send.at[c, 3])
+    for out in outs:
+        out.wait()
+
+
+def deliver(*refs):
+    sources, targets, held = refs[0:5], refs[5:10], refs[10:15]
+    in_sem, out_sem = refs[15:17]
+    ins = [pltpu.make_async_copy(sources[i], held[i], in_sem.at[i]) for i in range(5)]
+    outs = [pltpu.make_async_copy(held[i], targets[i], out_sem.at[i]) for i in range(5)]
+    for copy in ins:
+        copy.start()
+    for i in range(5):
+        ins[i].wait()
+        outs[i].start()
+    for copy in outs:
+        copy.wait()
 
 
 def body(tokens, grad_out, expert_ids, gates, w_gate, w_up, w_down):
@@ -427,17 +456,19 @@
     q1, q2, col = rows // 4, rows // 16, hid // 4
     packed = 3 * cap + cap // 2
     dma = pltpu.SemaphoreType.DMA
+    shapes = (
+        jax.ShapeDtypeStruct((feat, toks), BF16),
+        jax.ShapeDtypeStruct((feat, toks), BF16),
+        jax.ShapeDtypeStruct((feat, hid), BF16),
+        jax.ShapeDtypeStruct((feat, hid), BF16),
+        jax.ShapeDtypeStruct((feat, hid), BF16),
+    )
+    anywhere = pl.BlockSpec(memory_space=pl.ANY)
     results = pl.pallas_call(
         functools.partial(kernel, experts, cap, chunks),
-        out_shape=(
-            jax.ShapeDtypeStruct((feat, toks), BF16),
-            jax.ShapeDtypeStruct((feat, toks), BF16),
-            jax.ShapeDtypeStruct((feat, hid), BF16),
-            jax.ShapeDtypeStruct((feat, hid), BF16),
-            jax.ShapeDtypeStruct((feat, hid), BF16),
-        ),
-        in_specs=[pl.BlockSpec(memory_space=pltpu.VMEM)] * 7,
-        out_specs=(pl.BlockSpec(memory_space=pltpu.VMEM),) * 5,
+        out_shape=shapes,
+        in_specs=[pl.BlockSpec(memory_space=pltpu.VMEM)] * 4 + [anywhere] * 3,
+        out_specs=(anywhere,) * 5,
         scratch_shapes=[
             pltpu.VMEM((experts, packed, LANES), BF16),
             pltpu.VMEM((chunks, experts // chunks, packed, LANES), BF16),
@@ -457,9 +488,9 @@
             pltpu.VMEM((2 * LANES, hid), BF16),
             pltpu.VMEM((chunks, rows, 2 * LANES), BF16),
             pltpu.VMEM((chunks, rows, 2 * LANES), BF16),
-            pltpu.VMEM((2 * LANES, hid), F32),
-            pltpu.VMEM((2 * LANES, hid), F32),
-            pltpu.VMEM((2 * LANES, hid), F32),
+            *[pltpu.VMEM(shape.shape, BF16) for shape in shapes],
+            dma((5,)),
+            dma((5,)),
             dma,
             dma((chunks,)),
             dma,
@@ -476,7 +507,13 @@
             collective_id=0, has_side_effects=True, vmem_limit_bytes=60 * 1024 * 1024
         ),
     )(tokens.T, grad_out.T, expert_ids.T, gates.T, w_gate[0], w_up[0], w_down[0].T)
-    mixed, grad_tokens, grad_gate, grad_up, grad_down = results
+    mixed, grad_tokens, grad_gate, grad_up, grad_down = pl.pallas_call(
+        deliver,
+        out_shape=shapes,
+        in_specs=[anywhere] * 5,
+        out_specs=(anywhere,) * 5,
+        scratch_shapes=[pltpu.VMEM(shape.shape, BF16) for shape in shapes] + [dma((5,)), dma((5,))],
+    )(*results)
     return (mixed.T, grad_tokens.T, grad_gate[None], grad_up[None], grad_down.T[None])
 
 

time: 132 us -> 126 us (0.955)
  local copies, waits for them, and re-layouts: 5.54 us -> 0 us
    unnamed x13 -> x0, local copies, waits for them, and re-layouts: 5.54 us -> none
    pallas_call x1, Pallas kernels: 126 us -> 123 us  [body(): pl.pallas_call(functools.partial(kernel, experts, cap, chunks), out_shape...]
    pallas_call x0 -> x1, Pallas kernels: none -> 2.41 us  [body(): pl.pallas_call(deliver, out_shape=shapes, in_specs=[anywhere] * 5, out_sp...]
where the time goes in v3:
time: 126 us
  Pallas kernels  125 us (99%)
    pallas_call x1, Pallas kernels, body(): pl.pallas_call(functools.partial(kernel, experts, cap, chunks), out_shape...  123 us

profile of v3, /device:TPU:1, one launch (start us, length us, event | category | flops | bytes accessed | tf_op | source)
XLA Modules:
  0.0 125.6 jit_solution(16048438446043556144)
XLA Ops:
  0.6 122.6 %shard_map.110 = (bf16[224,512]{1,0:T(8,128)(2,1)}, bf16[224,512]{1,0:T(8,128)(2,1)}, bf16[224,1024]{1,0:T(8,128)(2,1)}, bf16[224,1024]{1,0:T(8,128)(2,1)}, bf16[224,1024]{1,0:T(8,128)(2,1)}) custom-call(bf16[224,512]{1,0:T(8,128)(2,1)} %bitcast.19, bf16[224,512]{1,0:T(8,128)(2,1)} %bitcast.20, s32[8,512]{1,0:T(8,128)} %bitcast.21, f32[8,512]{1,0:T(8,128)} %bitcast.22, ...), custom_call_target="tpu_custom_call" | custom-call | tf_op jit(solution)/shard_map/pallas_call | solution.py:467
  123.2 2.4 %shard_map.111 = (bf16[224,512]{1,0:T(8,128)(2,1)}, bf16[224,512]{1,0:T(8,128)(2,1)}, bf16[224,1024]{1,0:T(8,128)(2,1)}, bf16[224,1024]{1,0:T(8,128)(2,1)}, bf16[224,1024]{1,0:T(8,128)(2,1)}) custom-call(bf16[224,512]{1,0:T(8,128)(2,1)} %get-tuple-element.15.refs_0_, bf16[224,512]{1,0:T(8,128)(2,1)} %get-tuple-element.16.refs_1_, ...), custom_call_target="tpu_custom_call" | custom-call | tf_op jit(solution)/shard_map/pallas_call | solution.py:510

commit v4 on v3

--- a/solution.py
+++ b/solution.py
@@ -161,8 +161,6 @@
     counts = dot(one_hot.astype(BF16), earlier, ((1,), (0,)))
     position = jnp.sum(counts * one_hot, axis=0, keepdims=True)
     slot = jnp.where(routed > 0.0, chosen * cap + position, 2.0 * slots)
-    row_s = lax.broadcasted_iota(jnp.int32, (slots, toks), 0).astype(F32)
-    place[...] = jnp.where(row_s == slot, 1.0, 0.0).astype(BF16)
     scaled = (weight * gout_ref[...].astype(F32)).astype(BF16)
     comb[0:LANES, :] = tok_ref[0:LANES, :]
     comb[LANES : 2 * LANES, :] = scaled[0:LANES, :]
@@ -170,30 +168,45 @@
     comb[2 * LANES + wide : 3 * LANES, :] = scaled[LANES:cut, :]
     comb[3 * LANES : 3 * LANES + feat - cut, :] = scaled[cut:feat, :]
     comb[3 * LANES + feat - cut : 4 * LANES, :] = scaled[cut:feat, :]
-    laid = dot(place[...], comb[...], ((1,), (1,)))
-    for i in range(3):
-        send[:, i * cap : (i + 1) * cap, :] = (
-            laid[:, i * LANES : (i + 1) * LANES].astype(BF16).reshape(experts, cap, LANES)
-        )
-    last = laid[:, 3 * LANES : 4 * LANES].reshape(experts, cap, LANES)
     half = cap // 2
     lane = lax.broadcasted_iota(jnp.int32, (1, 1, LANES), 2)
-    send[:, 3 * cap : 3 * cap + half, :] = jnp.where(
-        lane < LANES // 2, last[:, 0:half, :], last[:, half:cap, :]
-    ).astype(BF16)
-
-    pl.semaphore_wait(barrier, 2 * zs - 1 + 4)
-
-    for c in range(chunks):
-        for j in range(per):
-            for dc in range(2):
-                dz = distance(c, j)
-                target = recv.at[c, 2 * j + dc]
-                if dz == 0 and dc == 0:
-                    pltpu.make_async_copy(send.at[me], target, disp_recv.at[c]).start()
+    row = lax.broadcasted_iota(jnp.int32, (cap, toks), 0).astype(F32)
+
+    def partner(c, k):
+        return peer(zs - distance(c, k // 2), k % 2)
+
+    def dispatch(low, high):
+        for i in range(low * blocks, high * blocks):
+            start = partner(i // blocks, i % blocks) * cap
+            place[i * cap : (i + 1) * cap, :] = jnp.where(
+                row == slot - start.astype(F32), 1.0, 0.0
+            ).astype(BF16)
+        count = (high - low) * blocks
+        here = slice(low * blocks, high * blocks)
+        laid = dot(place[low * rows : high * rows, :], comb[...], ((1,), (1,)))
+        for i in range(3):
+            send[here, i * cap : (i + 1) * cap, :] = (
+                laid[:, i * LANES : (i + 1) * LANES].astype(BF16).reshape(count, cap, LANES)
+            )
+        last = laid[:, 3 * LANES : 4 * LANES].reshape(count, cap, LANES)
+        send[here, 3 * cap : 3 * cap + half, :] = jnp.where(
+            lane < LANES // 2, last[:, 0:half, :], last[:, half:cap, :]
+        ).astype(BF16)
+        if low == 0:
+            pl.semaphore_wait(barrier, 2 * zs - 1 + 4)
+        for c in range(low, high):
+            for k in range(blocks):
+                source, target = send.at[c * blocks + k], recv.at[c, k]
+                if c == 0 and k == 0:
+                    pltpu.make_async_copy(source, target, disp_recv.at[c]).start()
                 else:
-                    there = peer(zs - dz, dc)
-                    z_send(send.at[there], target, disp_send, disp_recv.at[c], (dp, there))
+                    there = partner(c, k)
+                    z_send(source, target, disp_send, disp_recv.at[c], (dp, there))
+
+    near = min(2, chunks)
+    dispatch(0, near)
+    if near < chunks:
+        dispatch(near, chunks)
 
     def unpack(rows3, count):
         first_x = rows3[:, 0:cap, :]
@@ -349,11 +362,11 @@
 
         def go(k):
             there = peer(distance(c, k // 2), k % 2)
-            z_send(ret.at[c, k], back.at[me], back_send, back_recv, (dp, there))
+            z_send(ret.at[c, k], back.at[c * blocks + k], back_send, back_recv.at[c], (dp, there))
 
         @pl.when(c == 0)
         def _():
-            pltpu.make_async_copy(ret.at[c, 0], back.at[me], back_recv).start()
+            pltpu.make_async_copy(ret.at[c, 0], back.at[0], back_recv.at[c]).start()
 
         @pl.when(c > 0)
         def _():
@@ -412,12 +425,23 @@
 
     outs = [leave(0, out_g, ggate_ref), leave(1, out_u, gup_ref), leave(2, out_d, gdown_ref)]
 
-    z_wait(back, back_recv)
-    grad_pair, out_pair = unpack(back[...], experts)
     spots = ((0,), (0,))
-    restore(out_m, weight * dot(jnp.concatenate(out_pair, axis=1), place[...], spots))
+    early = max(chunks - 2, 1)
+    totals = []
+    for low, high in ((0, early), (early, chunks)):
+        for c in range(low, high):
+            z_wait(back.at[c * blocks : (c + 1) * blocks], back_recv.at[c])
+        grad_pair, out_pair = unpack(back[low * blocks : high * blocks], (high - low) * blocks)
+        spot = place[low * rows : high * rows, :]
+        totals.append(
+            (
+                dot(jnp.concatenate(out_pair, axis=1), spot, spots),
+                dot(jnp.concatenate(grad_pair, axis=1), spot, spots),
+            )
+        )
+    restore(out_m, weight * (totals[0][0] + totals[1][0]))
     outs.append(leave(3, out_m, mixed_ref))
-    out_t[...] = dot(jnp.concatenate(grad_pair, axis=1), place[...], spots)[0:feat].astype(BF16)
+    out_t[...] = (totals[0][1] + totals[1][1])[0:feat].astype(BF16)
     outs.append(leave(4, out_t, gtok_ref))
 
     z_wait(send.at[0 : experts - 1], disp_send)
@@ -494,7 +518,7 @@
             dma,
             dma((chunks,)),
             dma,
-            dma,
+            dma((chunks,)),
             dma((chunks, 4)),
             dma((chunks, 2, 2)),
             dma((chunks, 2)),

time: 126 us -> 126 us (level)
  no operation moved by 1% of the time
where the time goes in v4:
time: 126 us
  Pallas kernels  125 us (99%)
    pallas_call x1, Pallas kernels, body(): pl.pallas_call(functools.partial(kernel, experts, cap, chunks), out_shape...  123 us

profile of v4, /device:TPU:1, one launch (start us, length us, event | category | flops | bytes accessed | tf_op | source)
XLA Modules:
  0.0 125.6 jit_solution(14729105927080377837)
XLA Ops:
  0.6 122.6 %shard_map.110 = (bf16[224,512]{1,0:T(8,128)(2,1)}, bf16[224,512]{1,0:T(8,128)(2,1)}, bf16[224,1024]{1,0:T(8,128)(2,1)}, bf16[224,1024]{1,0:T(8,128)(2,1)}, bf16[224,1024]{1,0:T(8,128)(2,1)}) custom-call(bf16[224,512]{1,0:T(8,128)(2,1)} %bitcast.19, bf16[224,512]{1,0:T(8,128)(2,1)} %bitcast.20, s32[8,512]{1,0:T(8,128)} %bitcast.21, f32[8,512]{1,0:T(8,128)} %bitcast.22, ...), custom_call_target="tpu_custom_call" | custom-call | tf_op jit(solution)/shard_map/pallas_call | solution.py:491
  123.2 2.4 %shard_map.111 = (bf16[224,512]{1,0:T(8,128)(2,1)}, bf16[224,512]{1,0:T(8,128)(2,1)}, bf16[224,1024]{1,0:T(8,128)(2,1)}, bf16[224,1024]{1,0:T(8,128)(2,1)}, bf16[224,1024]{1,0:T(8,128)(2,1)}) custom-call(bf16[224,512]{1,0:T(8,128)(2,1)} %get-tuple-element.15.refs_0_, bf16[224,512]{1,0:T(8,128)(2,1)} %get-tuple-element.16.refs_1_, ...), custom_call_target="tpu_custom_call" | custom-call | tf_op jit(solution)/shard_map/pallas_call | solution.py:534

commit v5 on v4

--- a/solution.py
+++ b/solution.py
@@ -13,10 +13,17 @@
 RING = 4
 STARTS = (0, 1, 4, 5, 7, 8, 11, 12)
 LANES = 128
+NEARNESS = (0, 1, 3, 5, 7, 6, 4, 2)
 
 
 def dot(left, right, dims):
     return lax.dot_general(left, right, (dims, ((), ())), preferred_element_type=F32)
+
+
+def pick_from(table, index):
+    if isinstance(index, int):
+        return table[index]
+    return sum((index == i).astype(jnp.int32) * value for i, value in enumerate(table))
 
 
 def z_wait(ref, sem):
@@ -113,8 +120,7 @@
     def distance(c, j):
         base = per * c
         if chunks == len(STARTS):
-            late = c // (chunks // 2)
-            base = 2 * per * ((1 - late) * c + late * (chunks - 1 - c)) + late * per
+            base = per * pick_from(NEARNESS, c)
         k = base + j
         far, odd = (k + 1) // 2, k % 2
         return (odd * far + (1 - odd) * (zs - far)) % zs

time: 126 us -> 125 us (level)
    pallas_call x1, Pallas kernels: 123 us -> 121 us  [body(): pl.pallas_call(functools.partial(kernel, experts, cap, chunks), out_shape...]
where the time goes in v5:
time: 125 us; the launch traced here: 124 us
  Pallas kernels  124 us (99%)
    pallas_call x1, Pallas kernels, body(): pl.pallas_call(functools.partial(kernel, experts, cap, chunks), out_shape...  121 us

profile of v5, /device:TPU:1, one launch (start us, length us, event | category | flops | bytes accessed | tf_op | source)
XLA Modules:
  0.0 124.2 jit_solution(3428325507072385253)
XLA Ops:
  0.6 121.2 %shard_map.110 = (bf16[224,512]{1,0:T(8,128)(2,1)}, bf16[224,512]{1,0:T(8,128)(2,1)}, bf16[224,1024]{1,0:T(8,128)(2,1)}, bf16[224,1024]{1,0:T(8,128)(2,1)}, bf16[224,1024]{1,0:T(8,128)(2,1)}) custom-call(bf16[224,512]{1,0:T(8,128)(2,1)} %bitcast.19, bf16[224,512]{1,0:T(8,128)(2,1)} %bitcast.20, s32[8,512]{1,0:T(8,128)} %bitcast.21, f32[8,512]{1,0:T(8,128)} %bitcast.22, ...), custom_call_target="tpu_custom_call" | custom-call | tf_op jit(solution)/shard_map/pallas_call | solution.py:497
  121.8 2.4 %shard_map.111 = (bf16[224,512]{1,0:T(8,128)(2,1)}, bf16[224,512]{1,0:T(8,128)(2,1)}, bf16[224,1024]{1,0:T(8,128)(2,1)}, bf16[224,1024]{1,0:T(8,128)(2,1)}, bf16[224,1024]{1,0:T(8,128)(2,1)}) custom-call(bf16[224,512]{1,0:T(8,128)(2,1)} %get-tuple-element.15.refs_0_, bf16[224,512]{1,0:T(8,128)(2,1)} %get-tuple-element.16.refs_1_, ...), custom_call_target="tpu_custom_call" | custom-call | tf_op jit(solution)/shard_map/pallas_call | solution.py:540
